TPU v7x, 32 devices: a whole 2x2x4 slice. The times are simulated.
32 devices in a mesh: trial: 8 (over z, y), tensor: 4 (over x, core).
Axes of the slice: x: 2, y: 2, z: 4, core: 2. Of those that a mesh axis runs over, the one named last changes fastest.
Arguments:
- stored_attention: bfloat16 [8, 1024, 8192], P('trial', None, 'tensor'), may hold values from -6 to 6
- output_gradient: bfloat16 [8, 1024, 8192], P('trial', 'tensor'), may hold values from -6 to 6
- output_weight: bfloat16 [8192, 8192], P('tensor', 'trial'), may hold values from -0.0625 to 0.0625
- down_adapter: bfloat16 [8, 8192, 128], P('trial', 'tensor'), may hold values from -0.0625 to 0.0625
- up_adapter: bfloat16 [8, 128, 8192], P('trial'), may hold values from -0.0625 to 0.0625
- lengths: int32 [8], P('trial'), may hold values from 128 to 1024, as said below
- ranks: int32 [8], P('trial'), may hold values from 16 to 128, as said below
Outputs:
- attention_gradient: bfloat16 [8, 1024, 8192], P('trial', None, 'tensor')
- down_gradient: float32 [8, 8192, 128], P('trial', 'tensor')
- up_gradient: float32 [8, 128, 8192], P('trial', None, 'tensor')
Inputs may be any that keep to these rules, and one draw needn't show every extreme that they name: `lengths`: rows at or beyond a trial's count are padding; some trial has all 1024 rows live. `ranks`: each rank is a multiple of 16; some trial has rank 128 and some has 16.
All inputs are finite; a program needn't handle non-finite values.
Results may differ from a plain program's by a relative error of at most 0.0034.
Values may be sent and summed in bfloat16 or wider, within the bound.
A program may use at most 128 MiB of HBM per device.

v0:
```python
import jax
import jax.numpy as jnp
from jax import lax
from jax.sharding import PartitionSpec as P

adapter_alpha = 32.0


def row_product(left, right):
    return jnp.einsum("tk,hk->th", left, right, preferred_element_type=jnp.float32)


def body(
    stored_attention, output_gradient, output_weight, down_adapter, up_adapter, lengths, ranks
):
    attention_rows = stored_attention[0]
    gradient_rows = output_gradient[0]
    down_piece = down_adapter[0]
    up_complete = up_adapter[0]
    length = lengths[0]
    adapter_rank = ranks[0]
    token_rows = attention_rows.shape[0]
    head_cols = attention_rows.shape[1]
    shard_rows = gradient_rows.shape[0]
    rank_mask = jnp.arange(up_complete.shape[0]) < adapter_rank
    adapter_scale = adapter_alpha / jnp.sqrt(adapter_rank.astype(jnp.float32))
    a_low = jnp.where(rank_mask[None, :], down_piece, jnp.zeros_like(down_piece))
    b_low = jnp.where(rank_mask[:, None], up_complete, jnp.zeros_like(up_complete))
    row_offset = lax.axis_index("tensor") * shard_rows
    live_rows = row_offset + jnp.arange(shard_rows) < length
    gradient_rows = jnp.where(live_rows[:, None], gradient_rows, jnp.zeros_like(gradient_rows))
    u_part = jnp.einsum(
        "td,rd->tr", gradient_rows, b_low, preferred_element_type=jnp.float32
    ).astype(jnp.bfloat16)
    v_partial = jnp.dot(attention_rows, a_low, preferred_element_type=jnp.float32)
    lowrank_right = lax.psum(v_partial, "tensor").astype(jnp.bfloat16)
    col_start = lax.axis_index("tensor") * head_cols
    rows_all, u_all = (
        lax.all_gather(gradient_rows, "tensor", axis=0, tiled=True),
        lax.all_gather(u_part, "tensor", axis=0, tiled=True),
    )
    dense_piece = row_product(rows_all, lax.all_gather(output_weight, "trial", axis=1, tiled=True))
    lowrank_piece = jnp.einsum("tr,hr->th", u_all, a_low, preferred_element_type=jnp.float32)
    attention_gradient = (dense_piece + adapter_scale * lowrank_piece).astype(jnp.bfloat16)
    down_total = jnp.einsum("th,tr->hr", attention_rows, u_all, preferred_element_type=jnp.float32)
    own_cols = lax.dynamic_slice_in_dim(rows_all, col_start, head_cols, 1)
    up_total = jnp.einsum("tr,th->rh", lowrank_right, own_cols, preferred_element_type=jnp.float32)
    down_gradient = adapter_scale * down_total / float(token_rows)
    up_gradient = adapter_scale * up_total / float(token_rows)
    return (attention_gradient[None], down_gradient[None], up_gradient[None])


def solution(mesh):
    placed = (
        P("trial", None, "tensor"),
        P("trial", "tensor", None),
        P("tensor", "trial"),
        P("trial", "tensor", None),
        P("trial", None, None),
        P("trial"),
        P("trial"),
    )
    return jax.shard_map(
        body,
        mesh=mesh,
        in_specs=placed,
        out_specs=(
            P("trial", None, "tensor"),
            P("trial", "tensor", None),
            P("trial", None, "tensor"),
        ),
        check_vma=False,
    )
```

profile of v0, /device:TPU:0, one launch (start us, length us, event | category | flops | bytes accessed | tf_op | source)
XLA Modules:
  0.0 825.9 jit_solution(16108703871894892472)
XLA Ops:
  7.2 0.0 all-gather.3.cloned.1.call-start
  7.9 4.5 bitcast_select_fusion
  12.4 0.0 all-gather.3.cloned.1.call-update
  12.4 0.0 all-gather.5.cloned.1.call-start
  12.5 0.7 all-gather.5.cloned.1.call-update
  13.9 0.0 copy-start
  13.9 4.3 fusion.36
  18.2 0.0 copy-start.1
  18.3 7.3 all_gather.11
  25.6 0.0 copy-done
  25.6 0.7 fusion.20
  26.3 1.3 copy.10
  27.6 0.0 copy-done.1
  27.6 4.3 fusion.33
  32.0 26.7 %all-reduce.1 = bf16[1024,128]{0,1:T(8,128)(2,1)S(1)} all-reduce(f32[1024,128]{0,1:T(8,128)S(1)} %fusion.33), channel_id=1, replica_groups=mesh['trial'=8,'tensor'=4] {'tensor'}, use_global_device_ids=true, to_apply=%region_0.1 | all-reduce | flops 131072 | bytes 786432 | tf_op jit(solution)/shard_map/psum | solution.py:36
  58.7 71.0 %all-gather.3.cloned.1.call-done = bf16[1024,8192]{1,0:T(8,128)(2,1)} async-done(((bf16[256,8192]{1,0:T(8,128)(2,1)}), bf16[1024,8192]{1,0:T(8,128)(2,1)}) %all-gather.3.cloned.1.call-update) | async-done | bytes 16777232 | tf_op jit(solution)/shard_map/all_gather | solution.py:39
  129.6 3.9 fusion.26
  133.5 635.4 %all-gather.5.cloned.1.call-done = bf16[2048,8192]{1,0:T(8,128)(2,1)} async-done(((bf16[2048,1024]{1,0:T(8,128)(2,1)}), bf16[2048,8192]{1,0:T(8,128)(2,1)}) %all-gather.5.cloned.1.call-update) | async-done | bytes 33554448 | tf_op jit(solution)/shard_map/all_gather | solution.py:42
  769.0 43.4 %fusion.53 = f32[1024,2048]{1,0:T(8,128)} fusion(bf16[1024,8192]{1,0:T(8,128)(2,1)} %all-gather.3.cloned.1.call-done, bf16[2048,8192]{1,0:T(8,128)(2,1)} %all-gather.5.cloned.1.call-done), kind=kOutput, calls=%fused_computation.40 | convolution fusion | flops 34359738368 | bytes 58720256 | tf_op jit(solution)/shard_map/tk,hk->th/dot_general | solution.py:10
  812.4 6.6 fusion.10
  (2 shorter events, 0.0 us)
Async XLA Ops:
  7.2 122.5 %all-gather.3.cloned.1.call-start = ((), (), s32[]{:S(2)}) async-start(), calls=%async_computation | async-start | bytes 20971520 | tf_op jit(solution)/shard_map/all_gather | solution.py:39
  12.4 756.5 %all-gather.5.cloned.1.call-start = ((), (), s32[]{:S(2)}) async-start(), calls=%async_computation.1 | async-start | bytes 37748736 | tf_op jit(solution)/shard_map/all_gather | solution.py:42
  13.9 11.7 %copy-start = (bf16[1,1024,2048]{2,1,0:T(8,128)(2,1)S(1)}, bf16[1,1024,2048]{2,1,0:T(8,128)(2,1)}, u32[]{:S(2)}) copy-start(bf16[1,1024,2048]{2,1,0:T(8,128)(2,1)} %param.7) | copy-start | bytes 12582916
  18.2 9.4 %copy-start.1 = (bf16[1,2048,128]{2,1,0:T(8,128)(2,1)S(1)}, bf16[1,2048,128]{2,1,0:T(8,128)(2,1)}, u32[]{:S(2)}) copy-start(bf16[1,2048,128]{2,1,0:T(8,128)(2,1)} %param.10) | copy-start | bytes 1572868
Sparse Core Ops, SparseCore 0:
  12.6 117.0 all-gather.2
  131.2 637.7 all-gather.4
where the time goes:
time: 826 us
  waiting for transfers between devices  707 us (86%)
  matrix products  63.4 us (8%)
  blocking collectives  34 us (4%)
  between operations  15.4 us (2%)
    all_gather x1, waiting for transfers between devices, body(): lax.all_gather(output_weight, 'trial', axis=1, tiled=True)  635 us
    all_gather x1, waiting for transfers between devices, body(): lax.all_gather(gradient_rows, 'tensor', axis=0, tiled=True)  71 us
    dot_general x1, matrix products, row_product(): jnp.einsum('tk,hk->th', left, right, preferred_element_type=jnp.float32)  43.4 us
    psum x1, blocking collectives, body(): lowrank_right = lax.psum(v_partial, 'tensor').astype(jnp.bfloat16)  26.7 us
  transfers between devices with their start and end apart: 2, of which 2 were waited for; matrix products, arithmetic and copies ran while one was open for 2% of the time, Pallas kernels for 0%

commit v1 on v0

--- a/solution.py
+++ b/solution.py
@@ -13,6 +13,28 @@
 def body(
     stored_attention, output_gradient, output_weight, down_adapter, up_adapter, lengths, ranks
 ):
+
+    def arrange_the_joints(vals, axis_key):
+        val = lax.axis_size(axis_key)
+        mat_out, fresh, e_next = (val, lax.axis_index(axis_key), vals.shape[1])
+        in_order = [(ii, (ii + 1) % mat_out) for ii in range(mat_out)]
+        nodes = [(ii, (ii - 1) % mat_out) for ii in range(mat_out)]
+        n_now = jnp.zeros((*vals.shape[:1], mat_out * e_next, *vals.shape[2:]), vals.dtype)
+        n_now = lax.dynamic_update_slice_in_dim(n_now, vals, fresh * e_next, axis=1)
+        now = base_arr = vals
+        y1 = mat_out // 2
+        for j0 in range(1, y1 + 1):
+            now = lax.ppermute(now, axis_key, in_order)
+            n_now = lax.dynamic_update_slice_in_dim(
+                n_now, now, (fresh - j0) % mat_out * e_next, axis=1
+            )
+            if j0 < mat_out - y1:
+                base_arr = lax.ppermute(base_arr, axis_key, nodes)
+                n_now = lax.dynamic_update_slice_in_dim(
+                    n_now, base_arr, (fresh + j0) % mat_out * e_next, axis=1
+                )
+        return n_now
+
     attention_rows = stored_attention[0]
     gradient_rows = output_gradient[0]
     down_piece = down_adapter[0]
@@ -39,7 +61,7 @@
         lax.all_gather(gradient_rows, "tensor", axis=0, tiled=True),
         lax.all_gather(u_part, "tensor", axis=0, tiled=True),
     )
-    dense_piece = row_product(rows_all, lax.all_gather(output_weight, "trial", axis=1, tiled=True))
+    dense_piece = row_product(rows_all, arrange_the_joints(output_weight, "trial"))
     lowrank_piece = jnp.einsum("tr,hr->th", u_all, a_low, preferred_element_type=jnp.float32)
     attention_gradient = (dense_piece + adapter_scale * lowrank_piece).astype(jnp.bfloat16)
     down_total = jnp.einsum("th,tr->hr", attention_rows, u_all, preferred_element_type=jnp.float32)

time: 826 us -> 715 us (0.87)
  waiting for transfers between devices: 707 us -> 539 us
  local copies, waits for them, and re-layouts: 1.32 us -> 49.5 us
  starting transfers between devices: 0.08 us -> 19.7 us
  blocking collectives: 34 us -> 23.6 us
    all_gather x1 -> x0, waiting for transfers between devices: 635 us -> none  [body(): lax.all_gather(output_weight, 'trial', axis=1, tiled=True)]
    ppermute x0 -> x7, waiting for transfers between devices: none -> 539 us  [the longest x4 539 us: arrange_the_joints(): now = lax.ppermute(now, axis_key, in_order)]
    all_gather x1, waiting for transfers between devices: 71 us -> 0.01 us  [body(): lax.all_gather(gradient_rows, 'tensor', axis=0, tiled=True)]
    dynamic_update_slice x0 -> x8, local copies, waits for them, and re-layouts: none -> 34.5 us  [the longest x4 18.4 us: arrange_the_joints(): lax.dynamic_update_slice_in_dim(n_now, now, (fresh - j0) % mat_out * e_ne...]
    ppermute x0 -> x7, starting transfers between devices: none -> 19.7 us  [the longest x4 10.5 us: arrange_the_joints(): now = lax.ppermute(now, axis_key, in_order)]
    broadcast_in_dim x0 -> x1, local copies, waits for them, and re-layouts: none -> 11.7 us  [arrange_the_joints(): jnp.zeros((*vals.shape[:1], mat_out * e_next, *vals.shape[2:]), vals.dtype)]
    psum x1, blocking collectives: 26.7 us -> 17.8 us  [body(): lowrank_right = lax.psum(v_partial, 'tensor').astype(jnp.bfloat16)]
  transfers between devices with their start and end apart: 2 -> 8, of which waited for: 2 -> 4; matrix products, arithmetic and copies ran while one was open for 2% -> 8% of each run, Pallas kernels for 0% -> 0%
where the time goes in v1:
time: 715 us; the launch traced here: 714 us
  waiting for transfers between devices  539 us (75%)
  matrix products  62.1 us (9%)
  local copies, waits for them, and re-layouts  49.5 us (7%)
  blocking collectives  23.6 us (3%)
  starting transfers between devices  19.7 us (3%)
  between operations  15.5 us (2%)
    ppermute x4, waiting for transfers between devices, arrange_the_joints(): now = lax.ppermute(now, axis_key, in_order)  539 us
    dot_general x1, matrix products, row_product(): jnp.einsum('tk,hk->th', left, right, preferred_element_type=jnp.float32)  45.1 us
    dynamic_update_slice x4, local copies, waits for them, and re-layouts, arrange_the_joints(): lax.dynamic_update_slice_in_dim(n_now, now, (fresh - j0) % mat_out * e_ne...  18.4 us
    psum x1, blocking collectives, body(): lowrank_right = lax.psum(v_partial, 'tensor').astype(jnp.bfloat16)  17.8 us
  transfers between devices with their start and end apart: 8, of which 4 were waited for; matrix products, arithmetic and copies ran while one was open for 8% of the time, Pallas kernels for 0%

profile of v1, /device:TPU:0, one launch (start us, length us, event | category | flops | bytes accessed | tf_op | source)
XLA Modules:
  0.0 714.0 jit_solution(16821542163314245398)
XLA Ops:
  7.2 0.0 all-gather.2.cloned.1.call-start
  7.9 4.5 bitcast_select_fusion
  12.4 0.0 copy-start.3
  12.4 0.0 all-gather.2.cloned.1.call-update
  12.4 3.0 collective-permute-start
  15.5 3.1 collective-permute-start.1
  18.6 176.9 %collective-permute-done = bf16[2048,1024]{1,0:T(8,128)(2,1)S(1)} collective-permute-done((bf16[2048,1024]{1,0:T(8,128)(2,1)}, bf16[2048,1024]{1,0:T(8,128)(2,1)S(1)}, u32[]{:S(2)}, u32[]{:S(2)}) %collective-permute-start) | collective-permute-done | bytes 4194336 | tf_op jit(solution)/shard_map/ppermute | solution.py:27
  195.5 0.0 copy-start.2
  195.5 2.0 copy-done.2
  197.5 2.4 collective-permute-start.2
  199.9 0.0 collective-permute-done.1
  199.9 3.0 collective-permute-start.3
  202.9 175.8 %collective-permute-done.2 = bf16[2048,1024]{1,0:T(8,128)(2,1)} collective-permute-done((bf16[2048,1024]{1,0:T(8,128)(2,1)S(1)}, bf16[2048,1024]{1,0:T(8,128)(2,1)}, u32[]{:S(2)}, u32[]{:S(2)}) %collective-permute-start.2) | collective-permute-done | bytes 4194336 | tf_op jit(solution)/shard_map/ppermute | solution.py:27
  378.7 2.6 collective-permute-start.4
  382.0 0.0 collective-permute-done.3
  382.0 3.1 collective-permute-start.5
  385.1 0.0 copy-done.3
  385.1 3.7 fusion.33
  388.8 0.0 copy-start
  388.8 171.1 %collective-permute-done.4 = bf16[2048,1024]{1,0:T(8,128)(2,1)} collective-permute-done((bf16[2048,1024]{1,0:T(8,128)(2,1)}, bf16[2048,1024]{1,0:T(8,128)(2,1)}, u32[]{:S(2)}, u32[]{:S(2)}) %collective-permute-start.4) | collective-permute-done | bytes 4194336 | tf_op jit(solution)/shard_map/ppermute | solution.py:27
  559.9 2.5 collective-permute-start.6
  562.4 4.2 fusion.36
  566.6 5.8 all_gather.7
  572.4 0.0 copy-done
  572.4 0.7 fusion.20
  573.2 1.3 copy.10
  574.5 0.0 copy-start.1
  574.5 11.7 %broadcast_in_dim.58 = bf16[2048,8192]{1,0:T(8,128)(2,1)} broadcast(bf16[]{:T(256)} %constant.64.clone.1), dimensions={} | broadcast | bytes 33554432 | tf_op jit(solution)/shard_map/broadcast_in_dim | solution.py:22
  586.2 0.0 copy-done.1
  586.2 2.4 constant_dynamic-update-slice_fusion.7
  588.5 4.5 fusion.43
  593.0 17.8 %all-reduce.1 = bf16[1024,128]{0,1:T(8,128)(2,1)S(1)} all-reduce(f32[1024,128]{0,1:T(8,128)S(1)} %fusion.33), channel_id=1, replica_groups=mesh['trial'=8,'tensor'=4] {'tensor'}, use_global_device_ids=true, to_apply=%region_0.1 | all-reduce | flops 131072 | bytes 786432 | tf_op jit(solution)/shard_map/psum | solution.py:58
  610.9 4.6 constant_dynamic-update-slice_fusion.6
  615.4 4.6 constant_dynamic-update-slice_fusion.5
  620.0 4.6 constant_dynamic-update-slice_fusion.4
  624.5 4.6 constant_dynamic-update-slice_fusion.3
  629.1 4.6 constant_dynamic-update-slice_fusion.2
  633.7 0.0 collective-permute-done.5
  633.7 4.6 constant_dynamic-update-slice_fusion.1
  638.3 15.2 %collective-permute-done.6 = bf16[2048,1024]{1,0:T(8,128)(2,1)} collective-permute-done((bf16[2048,1024]{1,0:T(8,128)(2,1)}, bf16[2048,1024]{1,0:T(8,128)(2,1)}, u32[]{:S(2)}, u32[]{:S(2)}) %collective-permute-start.6) | collective-permute-done | bytes 4194336 | tf_op jit(solution)/shard_map/ppermute | solution.py:27
  653.5 4.6 constant_dynamic-update-slice_fusion
  658.2 0.0 all-gather.2.cloned.1.call-done
  658.2 45.1 %fusion = bf16[1,1024,2048]{2,1,0:T(8,128)(2,1)} fusion(f32[1024,2048]{1,0:T(8,128)} %fusion.43, f32[]{:T(128)S(6)} %div.15, bf16[1024,8192]{1,0:T(8,128)(2,1)} %all-gather.2.cloned.1.call-done, bf16[2048,8192]{1,0:T(8,128)(2,1)} %constant_dynamic-update-slice_fusion), kind=kOutput, calls=%fused_computation.1 | convolution fusion | flops 34366029824 | bytes 62914564 | tf_op jit(solution)/shard_map/tk,hk->th/dot_general | solution.py:10
  703.3 3.9 fusion.26
  (2 shorter events, 0.0 us)
Async XLA Ops:
  7.2 651.0 %all-gather.2.cloned.1.call-start = ((), (), s32[]{:S(2)}) async-start(), calls=%async_computation | async-start | bytes 20971520 | tf_op jit(solution)/shard_map/all_gather | solution.py:61
  12.4 372.7 %copy-start.3 = (bf16[1,2048,128]{2,1,0:T(8,128)(2,1)S(1)}, bf16[1,2048,128]{2,1,0:T(8,128)(2,1)}, u32[]{:S(2)}) copy-start(bf16[1,2048,128]{2,1,0:T(8,128)(2,1)} %param.10) | copy-start | bytes 1572868
  12.4 183.0 %collective-permute-start = (bf16[2048,1024]{1,0:T(8,128)(2,1)}, bf16[2048,1024]{1,0:T(8,128)(2,1)S(1)}, u32[]{:S(2)}, u32[]{:S(2)}) collective-permute-start(bf16[2048,1024]{1,0:T(8,128)(2,1)} %param.9), channel_id=1, source_target_pairs={{0,4},{4,8},{8,12},{12,16},{16,20},{20,24},{24,28},{28,0},{1,5},{5... | collective-permute-start | bytes 12582920 | tf_op jit(solution)/shard_map/ppermute | solution.py:27
  15.5 184.4 %collective-permute-start.1 = (bf16[2048,1024]{1,0:T(8,128)(2,1)}, bf16[2048,1024]{1,0:T(8,128)(2,1)}, u32[]{:S(2)}, u32[]{:S(2)}) collective-permute-start(bf16[2048,1024]{1,0:T(8,128)(2,1)} %param.9), channel_id=1, source_target_pairs={{0,28},{4,0},{8,4},{12,8},{16,12},{20,16},{24,20},{28,24},{1,29},{... | collective-permute-start | bytes 12582920 | tf_op jit(solution)/shard_map/ppermute | solution.py:32
  195.5 2.0 copy-start.2
  197.5 181.2 %collective-permute-start.2 = (bf16[2048,1024]{1,0:T(8,128)(2,1)S(1)}, bf16[2048,1024]{1,0:T(8,128)(2,1)}, u32[]{:S(2)}, u32[]{:S(2)}) collective-permute-start(bf16[2048,1024]{1,0:T(8,128)(2,1)S(1)} %collective-permute-done), channel_id=1, source_target_pairs={{0,4},{4,8},{8,12},{12,16},{16,20},{20,24},{24,28},{28,0},{1,5},{5... | collective-permute-start | bytes 12582920 | tf_op jit(solution)/shard_map/ppermute | solution.py:27
  199.9 182.1 %collective-permute-start.3 = (bf16[2048,1024]{1,0:T(8,128)(2,1)}, bf16[2048,1024]{1,0:T(8,128)(2,1)}, u32[]{:S(2)}, u32[]{:S(2)}) collective-permute-start(bf16[2048,1024]{1,0:T(8,128)(2,1)} %collective-permute-done.1), channel_id=1, source_target_pairs={{0,28},{4,0},{8,4},{12,8},{16,12},{20,16},{24,20},{28,24},{1,29},{... | collective-permute-start | bytes 12582920 | tf_op jit(solution)/shard_map/ppermute | solution.py:32
  378.7 181.2 %collective-permute-start.4 = (bf16[2048,1024]{1,0:T(8,128)(2,1)}, bf16[2048,1024]{1,0:T(8,128)(2,1)}, u32[]{:S(2)}, u32[]{:S(2)}) collective-permute-start(bf16[2048,1024]{1,0:T(8,128)(2,1)} %collective-permute-done.2), channel_id=1, source_target_pairs={{0,4},{4,8},{8,12},{12,16},{16,20},{20,24},{24,28},{28,0},{1,5},{5... | collective-permute-start | bytes 12582920 | tf_op jit(solution)/shard_map/ppermute | solution.py:27
  382.0 251.7 %collective-permute-start.5 = (bf16[2048,1024]{1,0:T(8,128)(2,1)}, bf16[2048,1024]{1,0:T(8,128)(2,1)}, u32[]{:S(2)}, u32[]{:S(2)}) collective-permute-start(bf16[2048,1024]{1,0:T(8,128)(2,1)} %collective-permute-done.3), channel_id=1, source_target_pairs={{0,28},{4,0},{8,4},{12,8},{16,12},{20,16},{24,20},{28,24},{1,29},{... | collective-permute-start | bytes 12582920 | tf_op jit(solution)/shard_map/ppermute | solution.py:32
  388.8 183.6 %copy-start = (bf16[1,1024,2048]{2,1,0:T(8,128)(2,1)S(1)}, bf16[1,1024,2048]{2,1,0:T(8,128)(2,1)}, u32[]{:S(2)}) copy-start(bf16[1,1024,2048]{2,1,0:T(8,128)(2,1)} %param.7) | copy-start | bytes 12582916
  559.9 93.6 %collective-permute-start.6 = (bf16[2048,1024]{1,0:T(8,128)(2,1)}, bf16[2048,1024]{1,0:T(8,128)(2,1)}, u32[]{:S(2)}, u32[]{:S(2)}) collective-permute-start(bf16[2048,1024]{1,0:T(8,128)(2,1)} %collective-permute-done.4), channel_id=1, source_target_pairs={{0,4},{4,8},{8,12},{12,16},{16,20},{20,24},{24,28},{28,0},{1,5},{5... | collective-permute-start | bytes 12582920 | tf_op jit(solution)/shard_map/ppermute | solution.py:27
  574.5 11.7 %copy-start.1 = (bf16[2048,1024]{1,0:T(8,128)(2,1)S(1)}, bf16[2048,1024]{1,0:T(8,128)(2,1)}, u32[]{:S(2)}) copy-start(bf16[2048,1024]{1,0:T(8,128)(2,1)} %param.9) | copy-start | bytes 12582916
Sparse Core Ops, SparseCore 0:
  12.6 108.6 all-gather.1
